TPU v7x, 128 devices: a whole 4x4x4 slice. The times are simulated.
128 devices in a mesh: dom: 16 (over z, y), qgrp: 8 (over x, core).
Axes of the slice: x: 4, y: 4, z: 4, core: 2. Of those that a mesh axis runs over, the one named last changes fastest.
Arguments:
- pair_state: bfloat16 [4096, 16384], P('dom', 'qgrp'), may hold values from -6 to 6
- cotangent: bfloat16 [4096, 16384], P('dom', 'qgrp'), may hold values from -6 to 6
- msg_weight: bfloat16 [2, 128, 128], replicated, may hold values from -0.5 to 0.5
- self_weight: bfloat16 [2, 128, 128], replicated, may hold values from -0.5 to 0.5
- pre_bias: float32 [2, 128], replicated, may hold values from -4 to 4
- norm_gain: float32 [2, 128], replicated, may hold values from 0.1 to 1.9
- rel_embed: bfloat16 [2, 822, 128], replicated, may hold values from -2 to 2
- rel_ids: int32 [4096, 8], P('dom'), may hold values from 0 to 821
- neighbours: int32 [4096, 8], P('dom'), may hold values from 0 to 384, as said below
- border: int32 [16, 16], P('dom'), may hold values from 0 to 255, as said below
- send_list: int32 [16, 16, 8], P('dom'), may hold values from 0 to 16, as said below
Outputs:
- final_state: bfloat16 [4096, 16384], P('dom', 'qgrp')
- grad_msg: float32 [2, 128, 128], replicated
- grad_self: float32 [2, 128, 128], replicated
- grad_bias: float32 [2, 128], replicated
- grad_gain: float32 [2, 128], replicated
- grad_rel: float32 [2, 822, 128], replicated
Inputs may be any that keep to these rules, and one draw needn't show every extreme that they name: `neighbours`: row v of partition d lists its incoming edges: n below 256 is row n of the same partition; 256 + p * 8 + j, with p not d and j below the count of send_list[p, d], is the j-th row that p sends to d; 384 is an empty slot. Each row has 1 to 8 edges, empty slots last. `border`: the 16 boundary rows of a partition are distinct rows of that partition. send_list[p, d] holds count distinct indices into border[p], then the value 16; count is 0 for d = p, 8 for d = (p + 1) mod 16, and 1 to 8 otherwise.
All inputs are finite; a program needn't handle non-finite values.
Results may differ from a plain program's by a relative error of at most 0.0061.
Values may be sent and summed in bfloat16 or wider, within the bound.
A program may use at most 128 MiB of HBM per device.

v0:
```python
import functools

import jax
import jax.numpy as jnp
from jax import lax
from jax.experimental import pallas as pl
from jax.experimental.pallas import tpu as pltpu
from jax.sharding import PartitionSpec as P

MESH = pl.DeviceIdType.MESH
F32 = jnp.float32
BF16 = jnp.bfloat16
WIDE = 256


def dot(a, b):
    return jnp.dot(a, b, preferred_element_type=F32)


def dot_nt(a, b):
    return lax.dot_general(a, b, (((1,), (1,)), ((), ())), preferred_element_type=F32)


def dot_tn(a, b):
    return lax.dot_general(a, b, (((0,), (0,)), ((), ())), preferred_element_type=F32)


def one_hot(ids, shape, axis):
    return jnp.where(lax.broadcasted_iota(jnp.int32, shape, axis) == ids, 1.0, 0.0).astype(BF16)


def split_parts(x):
    high = x.astype(BF16)
    low = (x - high.astype(F32)).astype(BF16)
    return jnp.concatenate([high, low], axis=1)


def fold_rows(x):
    return jnp.sum(x.reshape(x.shape[0] // 8, 8, x.shape[1]), axis=0)


def kernel(
    parts,
    groups,
    chunk,
    h_ref,
    cot_ref,
    wm_ref,
    ws_ref,
    bias_ref,
    gain_ref,
    rel_ref,
    relid_ref,
    nb_ref,
    rows_ref,
    final_ref,
    gm_ref,
    gs_ref,
    gb_ref,
    gg_ref,
    gr_ref,
    table,
    hot,
    hot_t,
    rel_t,
    factors,
    rel_cat,
    w_cat,
    ids,
    pick_t,
    kept0,
    kept1,
    contrib,
    xhat0,
    inv0,
    g1,
    agg,
    dagg,
    per_edge,
    grad_w,
    grad_b,
    grad_g,
    stage,
    back_in,
    ar_stage,
    ar_one,
    ar_two_stage,
    ar_two,
    ar_three_stage,
    ar_three,
    send_sems,
    recv_sems,
    ar_send,
    ar_recv,
    ar_send_q,
    ar_recv_q,
):
    me = lax.axis_index("dom")
    meq = lax.axis_index("qgrp")
    rows, features = h_ref.shape
    degree = nb_ref.shape[1]
    breadth = wm_ref.shape[1]
    rel_count = rel_ref.shape[1]
    half_cols = features // 2
    blocks = half_cols // WIDE
    slots = parts * 8
    edges = rows * degree
    rel_rows = rel_cat.shape[0]
    layers = 2
    queries = groups * (features // breadth)

    zero_land = jnp.zeros((slots, half_cols), BF16)
    for half in range(2):
        for layer in range(layers):
            table[layer, half, rows:, :] = zero_land
        back_in[half] = zero_land

    barrier = pltpu.get_barrier_semaphore()

    @pl.loop(1, parts)
    def _(i):
        pl.semaphore_signal(
            barrier, inc=1, device_id={"dom": lax.rem(me + i, parts)}, device_id_type=MESH
        )

    @pl.loop(1, groups)
    def _(i):
        pl.semaphore_signal(
            barrier, inc=1, device_id={"qgrp": lax.rem(meq + i, groups)}, device_id_type=MESH
        )

    pick_t[...] = one_hot(rows_ref[...], (rows, slots), 0)
    pick = jnp.transpose(
        jnp.where(
            lax.broadcasted_iota(jnp.int32, (rows, slots), 0) == rows_ref[...], 1.0, 0.0
        )
    ).astype(BF16)
    for half in range(2):
        stage[0, half] = dot(pick, h_ref[:, half * half_cols : (half + 1) * half_cols]).astype(BF16)

    pl.semaphore_wait(barrier, parts - 1 + groups - 1)

    def exchange(step, half, i, land):
        peer = lax.rem(me + i, parts)
        return pltpu.make_async_remote_copy(
            src_ref=stage.at[step, half, pl.ds(pl.multiple_of(peer * 8, 8), 8)],
            dst_ref=land(pl.multiple_of(me * 8, 8)),
            send_sem=send_sems.at[step, half, i],
            recv_sem=recv_sems.at[step, half, i],
            device_id={"dom": peer},
            device_id_type=MESH,
        )

    def landing(step, half):
        if step < 2:
            return lambda first: table.at[step, half, pl.ds(rows + first, 8)]
        return lambda first: back_in.at[half, pl.ds(first, 8)]

    def send(step, half):
        @pl.loop(1, parts)
        def _(i):
            exchange(step, half, i, landing(step, half)).start()

    def arrive(step, half):
        @pl.loop(1, parts)
        def _(i):
            exchange(step, half, i, landing(step, half)).wait_recv()

    def sent(step, half):
        @pl.loop(1, parts)
        def _(i):
            exchange(step, half, i, landing(step, half)).wait_send()

    send(0, 0)
    send(0, 1)

    for half in range(2):
        table[0, half, :rows, :] = h_ref[:, half * half_cols : (half + 1) * half_cols]
    ids[...] = jnp.zeros_like(ids)
    ids[:, :degree] = nb_ref[...]
    ids[:, degree : 2 * degree] = relid_ref[...]
    ids_t = jnp.transpose(ids[...])
    rel_cat[rel_rows - 96 :, :] = jnp.zeros((96, 2 * breadth), BF16)
    for layer in range(layers):
        rel_cat[:rel_count, layer * breadth : (layer + 1) * breadth] = rel_ref[layer]
        w_cat[layer, :breadth, :] = wm_ref[layer]
        w_cat[layer, breadth:, :] = ws_ref[layer]
    for k in range(degree):
        span = slice(k * rows, (k + 1) * rows)
        hot[span, :] = one_hot(nb_ref[:, k : k + 1], (rows, rows + slots), 1)
        hot_t[:, span] = one_hot(ids_t[k : k + 1, :], (rows + slots, rows), 0)
        rel_t[:, span] = one_hot(ids_t[degree + k : degree + k + 1, :], (rel_rows, rows), 0)
        factors[span, :] = dot(
            one_hot(relid_ref[:, k : k + 1], (rows, rel_rows), 1), rel_cat[...]
        ).astype(BF16)

    grad_w[...] = jnp.zeros_like(grad_w)
    grad_b[...] = jnp.zeros_like(grad_b)
    grad_g[...] = jnp.zeros_like(grad_g)
    per_edge[...] = jnp.zeros_like(per_edge)
    average = jnp.full((2 * breadth, breadth), 1.0 / breadth, BF16)

    def gather(layer, half, cols, kept, agg_cols):
        src = table[layer, half, :, cols]

        @pl.loop(0, degree)
        def _(k):
            span = pl.ds(pl.multiple_of(k * rows, rows), rows)
            kept[span, agg_cols if kept is kept0 else slice(None)] = dot(hot[span, :], src).astype(BF16)

        step = 32

        @pl.loop(0, rows // step)
        def _(r):
            total = None
            for k in range(degree):
                span = pl.ds(pl.multiple_of(k * rows + r * step, step), step)
                source = kept[span, agg_cols if kept is kept0 else slice(None)].astype(F32)
                factor = factors[span, layer * breadth : (layer + 1) * breadth].astype(F32)
                term = source * jnp.concatenate([factor] * (WIDE // breadth), axis=1)
                total = term if total is None else total + term
            agg[layer, pl.ds(pl.multiple_of(r * step, step), step), agg_cols] = total.astype(BF16)

    def forward(layer, x):
        pre = dot(x, w_cat[layer]) + bias_ref[layer : layer + 1, :]
        centre = pre - dot(split_parts(pre), average)
        var = dot((centre * centre).astype(BF16), average[:breadth])
        inv = lax.rsqrt(var + 1e-5)
        return centre * inv, inv

    def activate(layer, xhat):
        y = xhat * gain_ref[layer : layer + 1, :]
        return y, 0.5 * jnp.tanh(0.5 * y) + 0.5

    def backward(layer, up, x, xhat, inv, y, s):
        dy = up * s * (1.0 + y * (1.0 - s))
        dyx = dy * xhat
        grad_g[layer] += fold_rows(dyx)
        gain = gain_ref[layer : layer + 1, :]
        dx = dy * gain
        dxx = dyx * gain
        dpre = inv * (dx - dot(split_parts(dx), average) - xhat * dot(split_parts(dxx), average))
        grad_b[layer] += fold_rows(dpre)
        rounded = dpre.astype(BF16)
        grad_w[layer] += dot_tn(rounded, x)
        return dot_nt(rounded, w_cat[layer])

    def edge_products(kept, cols, layer):
        @pl.loop(0, degree)
        def _(k):
            span = pl.ds(pl.multiple_of(k * rows, rows), rows)
            source = kept[span, cols].astype(F32)
            product = source * dagg[...]
            total = product[:, :breadth]
            for part in range(1, WIDE // breadth):
                total = total + product[:, part * breadth : (part + 1) * breadth]
            per_edge[layer, span, :] += total

    for half in range(2):
        arrive(0, half)

        @pl.loop(0, blocks)
        def _(c):
            cols = pl.ds(pl.multiple_of(c * WIDE, WIDE), WIDE)
            wide = pl.ds(pl.multiple_of(half * half_cols + c * WIDE, WIDE), WIDE)
            gather(0, half, cols, kept0, wide)
            for part in range(WIDE // breadth):
                at = pl.ds(
                    pl.multiple_of(half * half_cols + c * WIDE + part * breadth, breadth), breadth
                )
                mine = pl.ds(pl.multiple_of(c * WIDE + part * breadth, breadth), breadth)
                state = h_ref[:, at]
                x = jnp.concatenate([agg[0, :, at], state], axis=1)
                xhat, inv = forward(0, x)
                xhat0[:, at] = xhat
                inv0[:, at] = inv
                y, s = activate(0, xhat)
                table[1, half, :rows, mine] = (state.astype(F32) + y * s).astype(BF16)

        stage[1, half] = dot(pick_to_rows(pick_t), table[1, half, :rows, :]).astype(BF16)
        send(1, half)

    for half in range(2):
        arrive(1, half)

        @pl.loop(0, blocks)
        def _(c):
            cols = pl.ds(pl.multiple_of(c * WIDE, WIDE), WIDE)
            wide = pl.ds(pl.multiple_of(half * half_cols + c * WIDE, WIDE), WIDE)
            gather(1, half, cols, kept1, wide)
            for part in range(WIDE // breadth):
                at = pl.ds(
                    pl.multiple_of(half * half_cols + c * WIDE + part * breadth, breadth), breadth
                )
                mine = pl.ds(pl.multiple_of(c * WIDE + part * breadth, breadth), breadth)
                state = table[1, half, :rows, mine]
                x = jnp.concatenate([agg[1, :, at], state], axis=1)
                xhat, inv = forward(1, x)
                y, s = activate(1, xhat)
                final_ref[:, at] = (state.astype(F32) + y * s).astype(BF16)
                up = cot_ref[:, at].astype(F32) * (1.0 / queries)
                both = backward(1, up, x, xhat, inv, y, s)
                dagg[:, part * breadth : (part + 1) * breadth] = both[:, :breadth]
                g1[:, at] = up + both[:, breadth:]
            edge_products(kept1, slice(None), 1)

            @pl.loop(0, degree)
            def _(k):
                span = pl.ds(pl.multiple_of(k * rows, rows), rows)
                factor = factors[span, breadth : 2 * breadth].astype(F32)
                contrib[span, :] = (
                    dagg[...] * jnp.concatenate([factor] * (WIDE // breadth), axis=1)
                ).astype(BF16)

            g1[:, wide] += dot(hot_t[:rows, :], contrib[...])
            stage[2, half, :, cols] = dot(hot_t[rows:, :], contrib[...]).astype(BF16)

        send(2, half)

    def gradients(layer):
        ar_stage[layer, :rel_rows, :] = dot(rel_t[...], per_edge[layer].astype(BF16)).astype(BF16)
        for part in range(2):
            first = rel_rows + part * breadth
            ar_stage[layer, first : first + breadth, :] = jnp.transpose(
                grad_w[layer, :, part * breadth : (part + 1) * breadth]
            ).astype(BF16)
        first = rel_rows + 2 * breadth
        ar_stage[layer, first : first + 16, :] = jnp.concatenate(
            [grad_b[layer], grad_g[layer]], axis=0
        ).astype(BF16)
        ar_stage[layer, first + 16 :, :] = jnp.zeros(
            (parts * chunk - first - 16, breadth), BF16
        )

    def scatter_sum(layer, i):
        peer = lax.rem(me + i, parts)
        return pltpu.make_async_remote_copy(
            src_ref=ar_stage.at[layer, pl.ds(pl.multiple_of(peer * chunk, 16), chunk)],
            dst_ref=ar_one.at[layer, me],
            send_sem=ar_send.at[layer, 0, i],
            recv_sem=ar_recv.at[layer, 0, i],
            device_id={"dom": peer},
            device_id_type=MESH,
        )

    def across(layer, i):
        return pltpu.make_async_remote_copy(
            src_ref=ar_two_stage.at[layer],
            dst_ref=ar_two.at[layer, meq],
            send_sem=ar_send_q.at[layer, i],
            recv_sem=ar_recv_q.at[layer, i],
            device_id={"qgrp": lax.rem(meq + i, groups)},
            device_id_type=MESH,
        )

    def spread(layer, i):
        return pltpu.make_async_remote_copy(
            src_ref=ar_three_stage.at[layer],
            dst_ref=ar_three.at[layer, pl.ds(pl.multiple_of(me * chunk, 16), chunk)],
            send_sem=ar_send.at[layer, 1, i],
            recv_sem=ar_recv.at[layer, 1, i],
            device_id={"dom": lax.rem(me + i, parts)},
            device_id_type=MESH,
        )

    def each(count, make, method):
        @pl.loop(1, count)
        def _(i):
            getattr(make(i), method)()

    def reduce_first(layer):
        ar_one[layer, me] = ar_stage[layer, pl.ds(pl.multiple_of(me * chunk, 16), chunk), :]
        each(parts, functools.partial(scatter_sum, layer), "start")

    def reduce_second(layer):
        each(parts, functools.partial(scatter_sum, layer), "wait_recv")
        total = ar_one[layer, 0].astype(F32)
        for p in range(1, parts):
            total = total + ar_one[layer, p].astype(F32)
        ar_two_stage[layer] = total.astype(BF16)
        ar_two[layer, meq] = total.astype(BF16)
        each(groups, functools.partial(across, layer), "start")

    def reduce_third(layer):
        each(groups, functools.partial(across, layer), "wait_recv")
        total = ar_two[layer, 0].astype(F32)
        for p in range(1, groups):
            total = total + ar_two[layer, p].astype(F32)
        ar_three_stage[layer] = total.astype(BF16)
        ar_three[layer, pl.ds(pl.multiple_of(me * chunk, 16), chunk), :] = total.astype(BF16)
        each(parts, functools.partial(spread, layer), "start")

    def reduce_finish(layer):
        each(parts, functools.partial(spread, layer), "wait_recv")
        gr_ref[layer] = ar_three[layer, :rel_count, :].astype(F32)
        gm_ref[layer] = ar_three[layer, rel_rows : rel_rows + breadth, :].astype(F32)
        gs_ref[layer] = ar_three[layer, rel_rows + breadth : rel_rows + 2 * breadth, :].astype(F32)
        first = rel_rows + 2 * breadth
        small = ar_three[layer, first : first + 16, :].astype(F32)
        gb_ref[layer : layer + 1, :] = jnp.sum(small[:8], axis=0, keepdims=True)
        gg_ref[layer : layer + 1, :] = jnp.sum(small[8:], axis=0, keepdims=True)
        each(parts, functools.partial(scatter_sum, layer), "wait_send")
        each(groups, functools.partial(across, layer), "wait_send")
        each(parts, functools.partial(spread, layer), "wait_send")

    gradients(1)
    reduce_first(1)

    for half in range(2):
        arrive(2, half)

        @pl.loop(0, blocks)
        def _(c):
            cols = pl.ds(pl.multiple_of(c * WIDE, WIDE), WIDE)
            wide = pl.ds(pl.multiple_of(half * half_cols + c * WIDE, WIDE), WIDE)
            g1[:, wide] += dot(pick_t[...], back_in[half, :, cols])
            for part in range(WIDE // breadth):
                at = pl.ds(
                    pl.multiple_of(half * half_cols + c * WIDE + part * breadth, breadth), breadth
                )
                x = jnp.concatenate([agg[0, :, at], h_ref[:, at]], axis=1)
                xhat = xhat0[:, at]
                y, s = activate(0, xhat)
                both = backward(0, g1[:, at], x, xhat, inv0[:, at], y, s)
                dagg[:, part * breadth : (part + 1) * breadth] = both[:, :breadth]
            edge_products(kept0, wide, 0)

        if half == 0:
            reduce_second(1)
        else:
            reduce_third(1)

    gradients(0)
    reduce_first(0)
    reduce_second(0)
    reduce_third(0)
    reduce_finish(1)
    reduce_finish(0)
    for step in range(3):
        for half in range(2):
            sent(step, half)


def pick_to_rows(pick_t):
    return jnp.transpose(pick_t[...].astype(F32)).astype(BF16)


def local(
    parts,
    groups,
    pair_state,
    cotangent,
    msg_weight,
    self_weight,
    pre_bias,
    norm_gain,
    rel_embed,
    rel_ids,
    neighbours,
    border,
    send_list,
):
    rows, features = pair_state.shape
    degree = neighbours.shape[1]
    layers, rel_count, breadth = rel_embed.shape
    slots = parts * 8
    half_cols = features // 2
    edges = rows * degree
    rel_rows = -(-rel_count // 128) * 128
    chunk = -(-(rel_rows + 2 * breadth + 16) // (parts * 16)) * 16
    total = parts * chunk
    kept = border.shape[1]
    match = send_list[0][:, :, None] == jnp.arange(kept, dtype=jnp.int32)
    chosen = jnp.sum(jnp.where(match, border[0] + 1, 0), axis=-1) - 1
    chosen = chosen.reshape(1, slots)
    vmem = pl.BlockSpec(memory_space=pltpu.VMEM)
    out_shape = [
        jax.ShapeDtypeStruct((rows, features), BF16),
        jax.ShapeDtypeStruct((layers, breadth, breadth), F32),
        jax.ShapeDtypeStruct((layers, breadth, breadth), F32),
        jax.ShapeDtypeStruct((layers, breadth), F32),
        jax.ShapeDtypeStruct((layers, breadth), F32),
        jax.ShapeDtypeStruct((layers, rel_count, breadth), F32),
    ]
    scratch = [
        pltpu.VMEM((layers, 2, rows + slots, half_cols), BF16),
        pltpu.VMEM((edges, rows + slots), BF16),
        pltpu.VMEM((rows + slots, edges), BF16),
        pltpu.VMEM((rel_rows, edges), BF16),
        pltpu.VMEM((edges, layers * breadth), BF16),
        pltpu.VMEM((rel_rows, layers * breadth), BF16),
        pltpu.VMEM((layers, 2 * breadth, breadth), BF16),
        pltpu.VMEM((rows, 128), jnp.int32),
        pltpu.VMEM((rows, slots), BF16),
        pltpu.VMEM((edges, features), BF16),
        pltpu.VMEM((edges, WIDE), BF16),
        pltpu.VMEM((edges, WIDE), BF16),
        pltpu.VMEM((rows, features), F32),
        pltpu.VMEM((rows, features), F32),
        pltpu.VMEM((rows, features), F32),
        pltpu.VMEM((layers, rows, features), BF16),
        pltpu.VMEM((rows, WIDE), F32),
        pltpu.VMEM((layers, edges, breadth), F32),
        pltpu.VMEM((layers, breadth, 2 * breadth), F32),
        pltpu.VMEM((layers, 8, breadth), F32),
        pltpu.VMEM((layers, 8, breadth), F32),
        pltpu.VMEM((3, 2, slots, half_cols), BF16),
        pltpu.VMEM((2, slots, half_cols), BF16),
        pltpu.VMEM((layers, total, breadth), BF16),
        pltpu.VMEM((layers, parts, chunk, breadth), BF16),
        pltpu.VMEM((layers, chunk, breadth), BF16),
        pltpu.VMEM((layers, groups, chunk, breadth), BF16),
        pltpu.VMEM((layers, chunk, breadth), BF16),
        pltpu.VMEM((layers, total, breadth), BF16),
        pltpu.SemaphoreType.DMA((3, 2, parts)),
        pltpu.SemaphoreType.DMA((3, 2, parts)),
        pltpu.SemaphoreType.DMA((layers, 2, parts)),
        pltpu.SemaphoreType.DMA((layers, 2, parts)),
        pltpu.SemaphoreType.DMA((layers, groups)),
        pltpu.SemaphoreType.DMA((layers, groups)),
    ]
    return tuple(
        pl.pallas_call(
            functools.partial(kernel, parts, groups, chunk),
            out_shape=out_shape,
            in_specs=[vmem] * 10,
            out_specs=[vmem] * 6,
            scratch_shapes=scratch,
            compiler_params=pltpu.CompilerParams(
                collective_id=0, has_side_effects=True, vmem_limit_bytes=67043328
            ),
            name="bellman_ford",
        )(
            pair_state,
            cotangent,
            msg_weight,
            self_weight,
            pre_bias,
            norm_gain,
            rel_embed,
            rel_ids,
            neighbours,
            chosen,
        )
    )


def solution(mesh):
    in_specs = (
        P("dom", "qgrp"),
        P("dom", "qgrp"),
        P(),
        P(),
        P(),
        P(),
        P(),
        P("dom", None),
        P("dom", None),
        P("dom", None),
        P("dom", None, None),
    )
    out_specs = (P("dom", "qgrp"), P(), P(), P(), P(), P())
    run = functools.partial(local, mesh.shape["dom"], mesh.shape["qgrp"])
    return jax.shard_map(run, mesh=mesh, in_specs=in_specs, out_specs=out_specs, check_vma=False)
```

profile of v0, /device:TPU:1, one launch (start us, length us, event | category | flops | bytes accessed | tf_op | source)
XLA Modules:
  0.0 128.9 jit_solution(14375767426349611257)
XLA Ops:
  0.6 0.0 copy-start.7
  0.6 0.6 copy-done.7
  1.3 0.8 copy.27
  2.0 0.4 select_reduce_fusion
  2.5 0.0 copy-start.3
  2.5 0.6 sub.7.rows_ref
  3.1 0.1 copy-done.3
  3.2 0.8 copy.29.relid_ref
  4.0 0.0 copy-done.4
  4.0 0.8 copy.30.nb_ref
  4.8 1.8 %copy.28.rel_ref = bf16[2,822,128]{2,1,0:T(8,128)(2,1)} copy(bf16[2,822,128]{2,0,1:T(2,128)(2,1)} %param.17) | data formatting | bytes 841728 | tf_op args[6]
  6.6 115.9 %bellman_ford.1 = (bf16[256,2048]{1,0:T(8,128)(2,1)}, f32[2,128,128]{2,1,0:T(8,128)}, f32[2,128,128]{2,1,0:T(8,128)}, f32[2,128]{1,0:T(2,128)}, f32[2,128]{1,0:T(2,128)}, /*index=5*/f32[2,822,128]{2,1,0:T(8,128)}) custom-call(bf16[256,2048]{1,0:T(8,128)(2,1)} %h_ref.1, bf16[256,2048]{1,0:T(8,128)(2,1)} %cot_ref.1, bf16[2,128,128]{2,1,0:T(8,128)(2,1)} %wm_ref.1, ...), custom_call_target="tpu_custom_call" | custom-call | tf_op jit(solution)/shard_map/bellman_ford/pallas_call | solution.py:523
  122.5 0.0 copy-start
  122.5 2.6 %copy.31 = f32[2,822,128]{2,0,1:T(2,128)} copy(f32[2,822,128]{2,1,0:T(8,128)} %get-tuple-element.23) | data formatting | bytes 1683456 | tf_op jit(solution)/shard_map/bellman_ford/pallas_call | solution.py:523
  125.0 0.0 copy-done
  125.0 1.0 copy.37
  126.0 0.1 copy-done.2
  126.1 0.7 copy.38
  126.7 0.3 copy-done.1
  127.0 0.7 copy.39
  127.7 0.0 copy-done.6
  127.7 0.6 copy.40
  128.3 0.1 copy-done.5
  128.4 0.6 copy.41
  (7 shorter events, 0.0 us)
Async XLA Ops:
  0.6 0.7 copy-start.7
  2.5 0.7 copy-start.3
  3.2 0.8 copy-start.4
  122.5 2.6 %copy-start = (bf16[256,2048]{1,0:T(8,128)(2,1)S(1)}, bf16[256,2048]{1,0:T(8,128)(2,1)}, u32[]{:S(2)}) copy-start(bf16[256,2048]{1,0:T(8,128)(2,1)} %get-tuple-element.30) | copy-start | bytes 3145732
  125.0 1.0 copy-start.2
  126.1 1.0 copy-start.1
  127.0 0.7 copy-start.6
  127.7 0.7 copy-start.5
where the time goes:
time: 129 us
  Pallas kernels  116 us (90%)
  local copies, waits for them, and re-layouts  11.9 us (9%)
    pallas_call x1, Pallas kernels, local(): pl.pallas_call(functools.partial(kernel, parts, groups, chunk), out_shape...  116 us
    unnamed x24, local copies, waits for them, and re-layouts  8.01 us

commit v1 on v0

--- a/solution.py
+++ b/solution.py
@@ -11,6 +11,8 @@
 F32 = jnp.float32
 BF16 = jnp.bfloat16
 WIDE = 256
+STEP = 32
+TOGETHER = 8
 
 
 def dot(a, b):
@@ -29,10 +31,17 @@
     return jnp.where(lax.broadcasted_iota(jnp.int32, shape, axis) == ids, 1.0, 0.0).astype(BF16)
 
 
-def split_parts(x):
-    high = x.astype(BF16)
-    low = (x - high.astype(F32)).astype(BF16)
-    return jnp.concatenate([high, low], axis=1)
+def place(ids, shape, axis):
+    low = lax.broadcasted_iota(jnp.int32, shape, axis) == (ids & 127)
+    return jnp.where(low, ids >> 7, -1).astype(F32).astype(BF16)
+
+
+def tile_hot(placed, tile):
+    return jnp.where(placed == jnp.asarray(tile, BF16), jnp.ones_like(placed), jnp.zeros_like(placed))
+
+
+def mean_row(x):
+    return jnp.mean(x, axis=1, keepdims=True)
 
 
 def fold_rows(x):
@@ -66,7 +75,7 @@
     factors,
     rel_cat,
     w_cat,
-    ids,
+    pick,
     pick_t,
     kept0,
     kept1,
@@ -107,6 +116,8 @@
     edges = rows * degree
     rel_rows = rel_cat.shape[0]
     layers = 2
+    chunks = rows // STEP
+    group = degree * STEP
     queries = groups * (features // breadth)
 
     zero_land = jnp.zeros((slots, half_cols), BF16)
@@ -130,13 +141,13 @@
         )
 
     pick_t[...] = one_hot(rows_ref[...], (rows, slots), 0)
-    pick = jnp.transpose(
+    pick[...] = jnp.transpose(
         jnp.where(
             lax.broadcasted_iota(jnp.int32, (rows, slots), 0) == rows_ref[...], 1.0, 0.0
         )
     ).astype(BF16)
     for half in range(2):
-        stage[0, half] = dot(pick, h_ref[:, half * half_cols : (half + 1) * half_cols]).astype(BF16)
+        stage[0, half] = dot(pick[...], h_ref[:, half * half_cols : (half + 1) * half_cols]).astype(BF16)
 
     pl.semaphore_wait(barrier, parts - 1 + groups - 1)
 
@@ -176,55 +187,69 @@
 
     for half in range(2):
         table[0, half, :rows, :] = h_ref[:, half * half_cols : (half + 1) * half_cols]
-    ids[...] = jnp.zeros_like(ids)
-    ids[:, :degree] = nb_ref[...]
-    ids[:, degree : 2 * degree] = relid_ref[...]
-    ids_t = jnp.transpose(ids[...])
     rel_cat[rel_rows - 96 :, :] = jnp.zeros((96, 2 * breadth), BF16)
     for layer in range(layers):
         rel_cat[:rel_count, layer * breadth : (layer + 1) * breadth] = rel_ref[layer]
         w_cat[layer, :breadth, :] = wm_ref[layer]
         w_cat[layer, breadth:, :] = ws_ref[layer]
-    for k in range(degree):
-        span = slice(k * rows, (k + 1) * rows)
-        hot[span, :] = one_hot(nb_ref[:, k : k + 1], (rows, rows + slots), 1)
-        hot_t[:, span] = one_hot(ids_t[k : k + 1, :], (rows + slots, rows), 0)
-        rel_t[:, span] = one_hot(ids_t[degree + k : degree + k + 1, :], (rel_rows, rows), 0)
-        factors[span, :] = dot(
-            one_hot(relid_ref[:, k : k + 1], (rows, rel_rows), 1), rel_cat[...]
-        ).astype(BF16)
+    across_ids = jnp.zeros((group, 128), jnp.int32)
+    lanes = lax.broadcasted_iota(jnp.int32, (group, 128), 1)
+    for r in range(chunks):
+        span = slice(r * group, (r + 1) * group)
+        some = slice(r * STEP, (r + 1) * STEP)
+        near = jnp.concatenate(
+            [jnp.broadcast_to(nb_ref[some, k : k + 1], (STEP, 128)) for k in range(degree)], axis=0
+        )
+        kind = jnp.concatenate(
+            [jnp.broadcast_to(relid_ref[some, k : k + 1], (STEP, 128)) for k in range(degree)], axis=0
+        )
+        across_ids = jnp.where(lanes == r, near, across_ids)
+        across_ids = jnp.where(lanes == chunks + r, kind, across_ids)
+        placed = place(near, (group, 128), 1)
+        for tile in range((rows + slots) // 128):
+            hot[span, tile * 128 : (tile + 1) * 128] = tile_hot(placed, tile)
+        placed = place(kind, (group, 128), 1)
+        which = jnp.concatenate([tile_hot(placed, t) for t in range(rel_rows // 128)], axis=1)
+        factors[span, :] = dot(which, rel_cat[...]).astype(BF16)
+    down_ids = jnp.transpose(across_ids)
+    for r in range(chunks):
+        span = slice(r * group, (r + 1) * group)
+        placed = place(down_ids[r : r + 1, :], (128, group), 0)
+        for tile in range((rows + slots) // 128):
+            hot_t[tile * 128 : (tile + 1) * 128, span] = tile_hot(placed, tile)
+        placed = place(down_ids[chunks + r : chunks + r + 1, :], (128, group), 0)
+        for tile in range(rel_rows // 128):
+            rel_t[tile * 128 : (tile + 1) * 128, span] = tile_hot(placed, tile)
 
     grad_w[...] = jnp.zeros_like(grad_w)
     grad_b[...] = jnp.zeros_like(grad_b)
     grad_g[...] = jnp.zeros_like(grad_g)
     per_edge[...] = jnp.zeros_like(per_edge)
-    average = jnp.full((2 * breadth, breadth), 1.0 / breadth, BF16)
 
     def gather(layer, half, cols, kept, agg_cols):
         src = table[layer, half, :, cols]
 
-        @pl.loop(0, degree)
-        def _(k):
-            span = pl.ds(pl.multiple_of(k * rows, rows), rows)
-            kept[span, agg_cols if kept is kept0 else slice(None)] = dot(hot[span, :], src).astype(BF16)
-
-        step = 32
-
-        @pl.loop(0, rows // step)
-        def _(r):
-            total = None
-            for k in range(degree):
-                span = pl.ds(pl.multiple_of(k * rows + r * step, step), step)
-                source = kept[span, agg_cols if kept is kept0 else slice(None)].astype(F32)
-                factor = factors[span, layer * breadth : (layer + 1) * breadth].astype(F32)
-                term = source * jnp.concatenate([factor] * (WIDE // breadth), axis=1)
-                total = term if total is None else total + term
-            agg[layer, pl.ds(pl.multiple_of(r * step, step), step), agg_cols] = total.astype(BF16)
+        at = agg_cols if kept is kept0 else slice(None)
+        for first in range(0, chunks, TOGETHER):
+            found = dot(hot[first * group : (first + TOGETHER) * group, :], src)
+            for r in range(first, first + TOGETHER):
+                mine = found[(r - first) * group : (r - first + 1) * group]
+                span = slice(r * group, (r + 1) * group)
+                kept[span, at] = mine.astype(BF16)
+                total = None
+                for k in range(degree):
+                    edge = slice(r * group + k * STEP, r * group + (k + 1) * STEP)
+                    factor = factors[edge, layer * breadth : (layer + 1) * breadth].astype(F32)
+                    term = mine[k * STEP : (k + 1) * STEP] * jnp.concatenate(
+                        [factor] * (WIDE // breadth), axis=1
+                    )
+                    total = term if total is None else total + term
+                agg[layer, r * STEP : (r + 1) * STEP, agg_cols] = total.astype(BF16)
 
     def forward(layer, x):
         pre = dot(x, w_cat[layer]) + bias_ref[layer : layer + 1, :]
-        centre = pre - dot(split_parts(pre), average)
-        var = dot((centre * centre).astype(BF16), average[:breadth])
+        centre = pre - mean_row(pre)
+        var = mean_row(centre * centre)
         inv = lax.rsqrt(var + 1e-5)
         return centre * inv, inv
 
@@ -239,22 +264,28 @@
         gain = gain_ref[layer : layer + 1, :]
         dx = dy * gain
         dxx = dyx * gain
-        dpre = inv * (dx - dot(split_parts(dx), average) - xhat * dot(split_parts(dxx), average))
+        dpre = inv * (dx - mean_row(dx) - xhat * mean_row(dxx))
         grad_b[layer] += fold_rows(dpre)
         rounded = dpre.astype(BF16)
         grad_w[layer] += dot_tn(rounded, x)
         return dot_nt(rounded, w_cat[layer])
 
     def edge_products(kept, cols, layer):
-        @pl.loop(0, degree)
-        def _(k):
-            span = pl.ds(pl.multiple_of(k * rows, rows), rows)
-            source = kept[span, cols].astype(F32)
-            product = source * dagg[...]
-            total = product[:, :breadth]
-            for part in range(1, WIDE // breadth):
-                total = total + product[:, part * breadth : (part + 1) * breadth]
-            per_edge[layer, span, :] += total
+        @pl.loop(0, chunks)
+        def _(r):
+            grad = dagg[pl.ds(pl.multiple_of(r * STEP, STEP), STEP), :]
+            for k in range(degree):
+                span = pl.ds(pl.multiple_of(r * group + k * STEP, STEP), STEP)
+                product = kept[span, cols].astype(F32) * grad
+                total = product[:, :breadth]
+                for part in range(1, WIDE // breadth):
+                    total = total + product[:, part * breadth : (part + 1) * breadth]
+                per_edge[layer, span, :] += total
+                if layer == 1:
+                    factor = factors[span, breadth : 2 * breadth].astype(F32)
+                    contrib[span, :] = (
+                        grad * jnp.concatenate([factor] * (WIDE // breadth), axis=1)
+                    ).astype(BF16)
 
     for half in range(2):
         arrive(0, half)
@@ -273,11 +304,11 @@
                 x = jnp.concatenate([agg[0, :, at], state], axis=1)
                 xhat, inv = forward(0, x)
                 xhat0[:, at] = xhat
-                inv0[:, at] = inv
+                inv0[:, at] = jnp.broadcast_to(inv, (rows, breadth))
                 y, s = activate(0, xhat)
                 table[1, half, :rows, mine] = (state.astype(F32) + y * s).astype(BF16)
 
-        stage[1, half] = dot(pick_to_rows(pick_t), table[1, half, :rows, :]).astype(BF16)
+        stage[1, half] = dot(pick[...], table[1, half, :rows, :]).astype(BF16)
         send(1, half)
 
     for half in range(2):
@@ -304,14 +335,6 @@
                 g1[:, at] = up + both[:, breadth:]
             edge_products(kept1, slice(None), 1)
 
-            @pl.loop(0, degree)
-            def _(k):
-                span = pl.ds(pl.multiple_of(k * rows, rows), rows)
-                factor = factors[span, breadth : 2 * breadth].astype(F32)
-                contrib[span, :] = (
-                    dagg[...] * jnp.concatenate([factor] * (WIDE // breadth), axis=1)
-                ).astype(BF16)
-
             g1[:, wide] += dot(hot_t[:rows, :], contrib[...])
             stage[2, half, :, cols] = dot(hot_t[rows:, :], contrib[...]).astype(BF16)
 
@@ -439,10 +462,6 @@
     for step in range(3):
         for half in range(2):
             sent(step, half)
-
-
-def pick_to_rows(pick_t):
-    return jnp.transpose(pick_t[...].astype(F32)).astype(BF16)
 
 
 def local(
@@ -490,7 +509,7 @@
         pltpu.VMEM((edges, layers * breadth), BF16),
         pltpu.VMEM((rel_rows, layers * breadth), BF16),
         pltpu.VMEM((layers, 2 * breadth, breadth), BF16),
-        pltpu.VMEM((rows, 128), jnp.int32),
+        pltpu.VMEM((slots, rows), BF16),
         pltpu.VMEM((rows, slots), BF16),
         pltpu.VMEM((edges, features), BF16),
         pltpu.VMEM((edges, WIDE), BF16),

time: 129 us -> 110 us (0.85)
  Pallas kernels: 116 us -> 96.8 us
    pallas_call x1, Pallas kernels: 116 us -> 96.8 us  [local(): pl.pallas_call(functools.partial(kernel, parts, groups, chunk), out_shape...]
where the time goes in v1:
time: 110 us
  Pallas kernels  96.8 us (88%)
  local copies, waits for them, and re-layouts  11.9 us (11%)
    pallas_call x1, Pallas kernels, local(): pl.pallas_call(functools.partial(kernel, parts, groups, chunk), out_shape...  96.8 us
    unnamed x24, local copies, waits for them, and re-layouts  8.01 us
    pallas_call x1, local copies, waits for them, and re-layouts, local(): pl.pallas_call(functools.partial(kernel, parts, groups, chunk), out_shape...  2.57 us

profile of v1, /device:TPU:1, one launch (start us, length us, event | category | flops | bytes accessed | tf_op | source)
XLA Modules:
  0.0 109.8 jit_solution(9703157696408924620)
XLA Ops:
  0.6 0.0 copy-start.7
  0.6 0.6 copy-done.7
  1.3 0.8 copy.27
  2.0 0.4 select_reduce_fusion
  2.5 0.0 copy-start.3
  2.5 0.6 sub.7.rows_ref
  3.1 0.1 copy-done.3
  3.2 0.8 copy.29.relid_ref
  4.0 0.0 copy-done.4
  4.0 0.8 copy.30.nb_ref
  4.8 1.8 %copy.28.rel_ref = bf16[2,822,128]{2,1,0:T(8,128)(2,1)} copy(bf16[2,822,128]{2,0,1:T(2,128)(2,1)} %param.17) | data formatting | bytes 841728 | tf_op args[6]
  6.6 96.8 %bellman_ford.1 = (bf16[256,2048]{1,0:T(8,128)(2,1)}, f32[2,128,128]{2,1,0:T(8,128)}, f32[2,128,128]{2,1,0:T(8,128)}, f32[2,128]{1,0:T(2,128)}, f32[2,128]{1,0:T(2,128)}, /*index=5*/f32[2,822,128]{2,1,0:T(8,128)}) custom-call(bf16[256,2048]{1,0:T(8,128)(2,1)} %h_ref.1, bf16[256,2048]{1,0:T(8,128)(2,1)} %cot_ref.1, bf16[2,128,128]{2,1,0:T(8,128)(2,1)} %wm_ref.1, ...), custom_call_target="tpu_custom_call" | custom-call | tf_op jit(solution)/shard_map/bellman_ford/pallas_call | solution.py:542
  103.4 0.0 copy-start
  103.4 2.6 %copy.31 = f32[2,822,128]{2,0,1:T(2,128)} copy(f32[2,822,128]{2,1,0:T(8,128)} %get-tuple-element.23) | data formatting | bytes 1683456 | tf_op jit(solution)/shard_map/bellman_ford/pallas_call | solution.py:542
  106.0 0.0 copy-done
  106.0 1.0 copy.37
  106.9 0.1 copy-done.2
  107.0 0.7 copy.38
  107.6 0.3 copy-done.1
  107.9 0.7 copy.39
  108.6 0.0 copy-done.6
  108.6 0.6 copy.40
  109.2 0.1 copy-done.5
  109.3 0.6 copy.41
  (7 shorter events, 0.0 us)
Async XLA Ops:
  0.6 0.7 copy-start.7
  2.5 0.7 copy-start.3
  3.2 0.8 copy-start.4
  103.4 2.6 %copy-start = (bf16[256,2048]{1,0:T(8,128)(2,1)S(1)}, bf16[256,2048]{1,0:T(8,128)(2,1)}, u32[]{:S(2)}) copy-start(bf16[256,2048]{1,0:T(8,128)(2,1)} %get-tuple-element.30) | copy-start | bytes 3145732
  106.0 1.0 copy-start.2
  107.0 1.0 copy-start.1
  107.9 0.7 copy-start.6
  108.6 0.7 copy-start.5

commit v2 on v1

--- a/solution.py
+++ b/solution.py
@@ -12,7 +12,7 @@
 BF16 = jnp.bfloat16
 WIDE = 256
 STEP = 32
-TOGETHER = 8
+TOGETHER = 2
 
 
 def dot(a, b):
@@ -61,19 +61,17 @@
     rel_ref,
     relid_ref,
     nb_ref,
-    rows_ref,
+    border_ref,
+    send_ref,
     final_ref,
-    gm_ref,
-    gs_ref,
-    gb_ref,
-    gg_ref,
-    gr_ref,
+    grads_ref,
     table,
     hot,
     hot_t,
     rel_t,
     factors,
     rel_cat,
+    rel_wide,
     w_cat,
     pick,
     pick_t,
@@ -103,13 +101,16 @@
     ar_recv,
     ar_send_q,
     ar_recv_q,
+    cot_buf,
+    final_buf,
+    local_sems,
 ):
     me = lax.axis_index("dom")
     meq = lax.axis_index("qgrp")
     rows, features = h_ref.shape
-    degree = nb_ref.shape[1]
+    degree = nb_ref.shape[0]
     breadth = wm_ref.shape[1]
-    rel_count = rel_ref.shape[1]
+    rel_count = rel_ref.shape[0] // 2
     half_cols = features // 2
     blocks = half_cols // WIDE
     slots = parts * 8
@@ -120,6 +121,15 @@
     group = degree * STEP
     queries = groups * (features // breadth)
 
+    fetch = pltpu.make_async_copy(cot_ref, cot_buf, local_sems.at[0])
+    fetch.start()
+
+    def write_back(half):
+        cols = pl.ds(half * half_cols, half_cols)
+        return pltpu.make_async_copy(
+            final_buf.at[:, cols], final_ref.at[:, cols], local_sems.at[1 + half]
+        )
+
     zero_land = jnp.zeros((slots, half_cols), BF16)
     for half in range(2):
         for layer in range(layers):
@@ -140,12 +150,28 @@
             barrier, inc=1, device_id={"qgrp": lax.rem(meq + i, groups)}, device_id_type=MESH
         )
 
-    pick_t[...] = one_hot(rows_ref[...], (rows, slots), 0)
-    pick[...] = jnp.transpose(
-        jnp.where(
-            lax.broadcasted_iota(jnp.int32, (rows, slots), 0) == rows_ref[...], 1.0, 0.0
-        )
+    lane = lax.broadcasted_iota(jnp.int32, (8, slots), 1)
+    repeat = jnp.where(
+        lax.broadcasted_iota(jnp.int32, (8, slots), 0) == (lane & 7), 1.0, 0.0
     ).astype(BF16)
+    spread_list = dot_tn(send_ref[0].astype(F32).astype(BF16), repeat)
+    own = lax.broadcasted_iota(jnp.int32, (parts, slots), 0) == (
+        lax.broadcasted_iota(jnp.int32, (parts, slots), 1) >> 3
+    )
+    place_in_border = jnp.sum(jnp.where(own, spread_list, 0.0), axis=0, keepdims=True)
+    kept_rows = border_ref.shape[1]
+    chosen = jnp.where(
+        lax.broadcasted_iota(jnp.int32, (kept_rows, slots), 0).astype(F32) == place_in_border,
+        1.0,
+        0.0,
+    ).astype(BF16)
+    border_rows = jnp.broadcast_to((border_ref[...] + 1).astype(F32), (8, kept_rows)).astype(BF16)
+    sent_rows = dot(border_rows, chosen)[:1] - 1.0
+    spot = jnp.where(
+        lax.broadcasted_iota(jnp.int32, (rows, slots), 0).astype(F32) == sent_rows, 1.0, 0.0
+    )
+    pick_t[...] = spot.astype(BF16)
+    pick[...] = jnp.transpose(spot).astype(BF16)
     for half in range(2):
         stage[0, half] = dot(pick[...], h_ref[:, half * half_cols : (half + 1) * half_cols]).astype(BF16)
 
@@ -187,21 +213,32 @@
 
     for half in range(2):
         table[0, half, :rows, :] = h_ref[:, half * half_cols : (half + 1) * half_cols]
+    rel_wide[...] = rel_ref[...].astype(F32)
     rel_cat[rel_rows - 96 :, :] = jnp.zeros((96, 2 * breadth), BF16)
     for layer in range(layers):
-        rel_cat[:rel_count, layer * breadth : (layer + 1) * breadth] = rel_ref[layer]
+        rel_cat[:rel_count, layer * breadth : (layer + 1) * breadth] = rel_wide[
+            pl.ds(layer, rel_count, stride=2), :
+        ].astype(BF16)
         w_cat[layer, :breadth, :] = wm_ref[layer]
         w_cat[layer, breadth:, :] = ws_ref[layer]
+    down = jnp.concatenate(
+        [nb_ref[...], relid_ref[...], jnp.zeros((128 - 2 * degree, rows), jnp.int32)], axis=0
+    )
+    columns = jnp.transpose(down)
     across_ids = jnp.zeros((group, 128), jnp.int32)
     lanes = lax.broadcasted_iota(jnp.int32, (group, 128), 1)
     for r in range(chunks):
         span = slice(r * group, (r + 1) * group)
         some = slice(r * STEP, (r + 1) * STEP)
         near = jnp.concatenate(
-            [jnp.broadcast_to(nb_ref[some, k : k + 1], (STEP, 128)) for k in range(degree)], axis=0
+            [jnp.broadcast_to(columns[some, k : k + 1], (STEP, 128)) for k in range(degree)], axis=0
         )
         kind = jnp.concatenate(
-            [jnp.broadcast_to(relid_ref[some, k : k + 1], (STEP, 128)) for k in range(degree)], axis=0
+            [
+                jnp.broadcast_to(columns[some, degree + k : degree + k + 1], (STEP, 128))
+                for k in range(degree)
+            ],
+            axis=0,
         )
         across_ids = jnp.where(lanes == r, near, across_ids)
         across_ids = jnp.where(lanes == chunks + r, kind, across_ids)
@@ -311,6 +348,7 @@
         stage[1, half] = dot(pick[...], table[1, half, :rows, :]).astype(BF16)
         send(1, half)
 
+    fetch.wait()
     for half in range(2):
         arrive(1, half)
 
@@ -328,8 +366,8 @@
                 x = jnp.concatenate([agg[1, :, at], state], axis=1)
                 xhat, inv = forward(1, x)
                 y, s = activate(1, xhat)
-                final_ref[:, at] = (state.astype(F32) + y * s).astype(BF16)
-                up = cot_ref[:, at].astype(F32) * (1.0 / queries)
+                final_buf[:, at] = (state.astype(F32) + y * s).astype(BF16)
+                up = cot_buf[:, at].astype(F32) * (1.0 / queries)
                 both = backward(1, up, x, xhat, inv, y, s)
                 dagg[:, part * breadth : (part + 1) * breadth] = both[:, :breadth]
                 g1[:, at] = up + both[:, breadth:]
@@ -339,6 +377,7 @@
             stage[2, half, :, cols] = dot(hot_t[rows:, :], contrib[...]).astype(BF16)
 
         send(2, half)
+        write_back(half).start()
 
     def gradients(layer):
         ar_stage[layer, :rel_rows, :] = dot(rel_t[...], per_edge[layer].astype(BF16)).astype(BF16)
@@ -415,13 +454,7 @@
 
     def reduce_finish(layer):
         each(parts, functools.partial(spread, layer), "wait_recv")
-        gr_ref[layer] = ar_three[layer, :rel_count, :].astype(F32)
-        gm_ref[layer] = ar_three[layer, rel_rows : rel_rows + breadth, :].astype(F32)
-        gs_ref[layer] = ar_three[layer, rel_rows + breadth : rel_rows + 2 * breadth, :].astype(F32)
-        first = rel_rows + 2 * breadth
-        small = ar_three[layer, first : first + 16, :].astype(F32)
-        gb_ref[layer : layer + 1, :] = jnp.sum(small[:8], axis=0, keepdims=True)
-        gg_ref[layer : layer + 1, :] = jnp.sum(small[8:], axis=0, keepdims=True)
+        grads_ref[layer] = ar_three[layer]
         each(parts, functools.partial(scatter_sum, layer), "wait_send")
         each(groups, functools.partial(across, layer), "wait_send")
         each(parts, functools.partial(spread, layer), "wait_send")
@@ -462,6 +495,35 @@
     for step in range(3):
         for half in range(2):
             sent(step, half)
+    for half in range(2):
+        write_back(half).wait()
+
+
+def unpack(
+    final_in,
+    grads_in,
+    final_out,
+    gm_ref,
+    gs_ref,
+    gb_ref,
+    gg_ref,
+    gr_ref,
+    copy_sem,
+):
+    whole = pltpu.make_async_copy(final_in, final_out, copy_sem)
+    whole.start()
+    breadth = gm_ref.shape[1]
+    rel_count = gr_ref.shape[0] // 2
+    rel_rows = -(-rel_count // 128) * 128
+    for layer in range(2):
+        gr_ref[pl.ds(layer, rel_count, stride=2), :] = grads_in[layer, :rel_count, :].astype(F32)
+        gm_ref[layer] = grads_in[layer, rel_rows : rel_rows + breadth, :].astype(F32)
+        gs_ref[layer] = grads_in[layer, rel_rows + breadth : rel_rows + 2 * breadth, :].astype(F32)
+        first = rel_rows + 2 * breadth
+        small = grads_in[layer, first : first + 16, :].astype(F32)
+        gb_ref[layer : layer + 1, :] = jnp.sum(small[:8], axis=0, keepdims=True)
+        gg_ref[layer : layer + 1, :] = jnp.sum(small[8:], axis=0, keepdims=True)
+    whole.wait()
 
 
 def local(
@@ -488,18 +550,16 @@
     rel_rows = -(-rel_count // 128) * 128
     chunk = -(-(rel_rows + 2 * breadth + 16) // (parts * 16)) * 16
     total = parts * chunk
-    kept = border.shape[1]
-    match = send_list[0][:, :, None] == jnp.arange(kept, dtype=jnp.int32)
-    chosen = jnp.sum(jnp.where(match, border[0] + 1, 0), axis=-1) - 1
-    chosen = chosen.reshape(1, slots)
     vmem = pl.BlockSpec(memory_space=pltpu.VMEM)
+    anywhere = pl.BlockSpec(memory_space=pl.ANY)
+    grads_shape = jax.ShapeDtypeStruct((layers, total, breadth), BF16)
     out_shape = [
         jax.ShapeDtypeStruct((rows, features), BF16),
         jax.ShapeDtypeStruct((layers, breadth, breadth), F32),
         jax.ShapeDtypeStruct((layers, breadth, breadth), F32),
         jax.ShapeDtypeStruct((layers, breadth), F32),
         jax.ShapeDtypeStruct((layers, breadth), F32),
-        jax.ShapeDtypeStruct((layers, rel_count, breadth), F32),
+        jax.ShapeDtypeStruct((layers * rel_count, breadth), F32),
     ]
     scratch = [
         pltpu.VMEM((layers, 2, rows + slots, half_cols), BF16),
@@ -508,6 +568,7 @@
         pltpu.VMEM((rel_rows, edges), BF16),
         pltpu.VMEM((edges, layers * breadth), BF16),
         pltpu.VMEM((rel_rows, layers * breadth), BF16),
+        pltpu.VMEM((layers * rel_count, breadth), F32),
         pltpu.VMEM((layers, 2 * breadth, breadth), BF16),
         pltpu.VMEM((slots, rows), BF16),
         pltpu.VMEM((rows, slots), BF16),
@@ -537,31 +598,43 @@
         pltpu.SemaphoreType.DMA((layers, 2, parts)),
         pltpu.SemaphoreType.DMA((layers, groups)),
         pltpu.SemaphoreType.DMA((layers, groups)),
+        pltpu.VMEM((rows, features), BF16),
+        pltpu.VMEM((rows, features), BF16),
+        pltpu.SemaphoreType.DMA((3,)),
     ]
-    return tuple(
-        pl.pallas_call(
-            functools.partial(kernel, parts, groups, chunk),
-            out_shape=out_shape,
-            in_specs=[vmem] * 10,
-            out_specs=[vmem] * 6,
-            scratch_shapes=scratch,
-            compiler_params=pltpu.CompilerParams(
-                collective_id=0, has_side_effects=True, vmem_limit_bytes=67043328
-            ),
-            name="bellman_ford",
-        )(
-            pair_state,
-            cotangent,
-            msg_weight,
-            self_weight,
-            pre_bias,
-            norm_gain,
-            rel_embed,
-            rel_ids,
-            neighbours,
-            chosen,
-        )
+    final, grads = pl.pallas_call(
+        functools.partial(kernel, parts, groups, chunk),
+        out_shape=[out_shape[0], grads_shape],
+        in_specs=[vmem, anywhere] + [vmem] * 9,
+        out_specs=[anywhere, vmem],
+        scratch_shapes=scratch,
+        compiler_params=pltpu.CompilerParams(
+            collective_id=0, has_side_effects=True, vmem_limit_bytes=67043328
+        ),
+        name="bellman_ford",
+    )(
+        pair_state,
+        cotangent,
+        msg_weight,
+        self_weight,
+        pre_bias,
+        norm_gain,
+        jnp.transpose(rel_embed, (1, 0, 2)).reshape(layers * rel_count, breadth),
+        rel_ids.T,
+        neighbours.T,
+        border,
+        jnp.transpose(send_list, (0, 2, 1)),
     )
+    final, gm, gs, gb, gg, gr = pl.pallas_call(
+        unpack,
+        out_shape=out_shape,
+        in_specs=[vmem] * 2,
+        out_specs=[anywhere] + [vmem] * 5,
+        scratch_shapes=[pltpu.SemaphoreType.DMA],
+        compiler_params=pltpu.CompilerParams(vmem_limit_bytes=16 * 1024 * 1024),
+        name="unpack",
+    )(final, grads)
+    return final, gm, gs, gb, gg, jnp.transpose(gr.reshape(rel_count, layers, breadth), (1, 0, 2))
 
 
 def solution(mesh):

time: 110 us -> 94.8 us (0.86)
  Pallas kernels: 96.8 us -> 87.8 us
  local copies, waits for them, and re-layouts: 11.9 us -> 6.08 us
    pallas_call x1, Pallas kernels: 96.8 us -> 86.1 us  [local(): pl.pallas_call(functools.partial(kernel, parts, groups, chunk), out_shape...]
    unnamed x24 -> x4, local copies, waits for them, and re-layouts: 8.01 us -> 2.3 us
    reshape x0 -> x2, local copies, waits for them, and re-layouts: none -> 3.77 us  [the longest x1 2.38 us: local(): jnp.transpose(rel_embed, (1, 0, 2)).reshape(layers * rel_count, breadth)]
    pallas_call x1 -> x0, local copies, waits for them, and re-layouts: 2.57 us -> none  [local(): pl.pallas_call(functools.partial(kernel, parts, groups, chunk), out_shape...]
    pallas_call x0 -> x1, Pallas kernels: none -> 1.68 us  [local(): pl.pallas_call(unpack, out_shape=out_shape, in_specs=[vmem] * 2, out_spec...]
where the time goes in v2:
time: 94.8 us; the launch traced here: 94.5 us
  Pallas kernels  87.8 us (93%)
  local copies, waits for them, and re-layouts  6.08 us (6%)
    pallas_call x1, Pallas kernels, local(): pl.pallas_call(functools.partial(kernel, parts, groups, chunk), out_shape...  86.1 us
    reshape x1, local copies, waits for them, and re-layouts, local(): jnp.transpose(rel_embed, (1, 0, 2)).reshape(layers * rel_count, breadth)  2.38 us
    unnamed x4, local copies, waits for them, and re-layouts  2.3 us

profile of v2, /device:TPU:1, one launch (start us, length us, event | category | flops | bytes accessed | tf_op | source)
XLA Modules:
  0.0 94.5 jit_solution(16881160474819928372)
XLA Ops:
  0.6 2.4 %reshape.18.rel_ref = bf16[1644,128]{1,0:T(8,128)(2,1)} reshape(bf16[822,2,128]{2,1,0:T(2,128)(2,1)} %bitcast.6) | data formatting | bytes 841728 | tf_op jit(solution)/shard_map/reshape | solution.py:622
  3.0 86.1 %bellman_ford.1 = (bf16[256,2048]{1,0:T(8,128)(2,1)}, bf16[2,1280,128]{2,1,0:T(8,128)(2,1)}) custom-call(bf16[256,2048]{1,0:T(8,128)(2,1)} %h_ref.1, bf16[256,2048]{1,0:T(8,128)(2,1)} %cot_ref.1, bf16[2,128,128]{2,1,0:T(8,128)(2,1)} %wm_ref.1, bf16[2,128,128]{2,1,0:T(8,128)(2,1)} %ws_ref.1, f32[2,128]{1,0:T(2,128)} %bias_ref.1, f32[2,128]{1,0:T(2,128)} %gain_ref.1, ...), custom_call_target="tpu_custom_call" | custom-call | tf_op jit(solution)/shard_map/bellman_ford/pallas_call | solution.py:605
  89.1 0.0 copy-start
  89.1 1.2 %copy-done = bf16[256,2048]{1,0:T(8,128)(2,1)S(1)} copy-done((bf16[256,2048]{1,0:T(8,128)(2,1)S(1)}, bf16[256,2048]{1,0:T(8,128)(2,1)}, u32[]{:S(2)}) %copy-start) | copy-done | bytes 1048600
  90.3 0.0 copy-start.1
  90.3 1.1 %copy-done.1 = bf16[2,1280,128]{2,1,0:T(8,128)(2,1)S(1)} copy-done((bf16[2,1280,128]{2,1,0:T(8,128)(2,1)S(1)}, bf16[2,1280,128]{2,1,0:T(8,128)(2,1)}, u32[]{:S(2)}) %copy-start.1) | copy-done | bytes 655384
  91.4 1.7 %unpack.1 = (bf16[256,2048]{1,0:T(8,128)(2,1)}, f32[2,128,128]{2,1,0:T(8,128)}, f32[2,128,128]{2,1,0:T(8,128)}, f32[2,128]{1,0:T(2,128)}, f32[2,128]{1,0:T(2,128)}, /*index=5*/f32[1644,128]{1,0:T(8,128)S(1)}) custom-call(bf16[256,2048]{1,0:T(8,128)(2,1)S(1)} %copy-done, bf16[2,1280,128]{2,1,0:T(8,128)(2,1)S(1)} %copy-done.1), custom_call_target="tpu_custom_call" | custom-call | tf_op jit(solution)/shard_map/unpack/pallas_call | solution.py:628
  93.1 1.4 %reshape.19 = f32[822,2,128]{2,1,0:T(2,128)} reshape(f32[1644,128]{1,0:T(8,128)S(1)} %get-tuple-element.21) | data formatting | bytes 1683456 | tf_op jit(solution)/shard_map/reshape | solution.py:637
Async XLA Ops:
  89.1 1.2 %copy-start = (bf16[256,2048]{1,0:T(8,128)(2,1)S(1)}, bf16[256,2048]{1,0:T(8,128)(2,1)}, u32[]{:S(2)}) copy-start(bf16[256,2048]{1,0:T(8,128)(2,1)} %get-tuple-element.14.final_in) | copy-start | bytes 3145732
  90.3 1.1 %copy-start.1 = (bf16[2,1280,128]{2,1,0:T(8,128)(2,1)S(1)}, bf16[2,1280,128]{2,1,0:T(8,128)(2,1)}, u32[]{:S(2)}) copy-start(bf16[2,1280,128]{2,1,0:T(8,128)(2,1)} %get-tuple-element.15.grads_in) | copy-start | bytes 1966084

commit v3 on v2

--- a/solution.py
+++ b/solution.py
@@ -12,7 +12,7 @@
 BF16 = jnp.bfloat16
 WIDE = 256
 STEP = 32
-TOGETHER = 2
+TOGETHER = 4
 
 
 def dot(a, b):
@@ -71,7 +71,6 @@
     rel_t,
     factors,
     rel_cat,
-    rel_wide,
     w_cat,
     pick,
     pick_t,
@@ -110,7 +109,7 @@
     rows, features = h_ref.shape
     degree = nb_ref.shape[0]
     breadth = wm_ref.shape[1]
-    rel_count = rel_ref.shape[0] // 2
+    rel_count = rel_ref.shape[0]
     half_cols = features // 2
     blocks = half_cols // WIDE
     slots = parts * 8
@@ -213,12 +212,9 @@
 
     for half in range(2):
         table[0, half, :rows, :] = h_ref[:, half * half_cols : (half + 1) * half_cols]
-    rel_wide[...] = rel_ref[...].astype(F32)
     rel_cat[rel_rows - 96 :, :] = jnp.zeros((96, 2 * breadth), BF16)
     for layer in range(layers):
-        rel_cat[:rel_count, layer * breadth : (layer + 1) * breadth] = rel_wide[
-            pl.ds(layer, rel_count, stride=2), :
-        ].astype(BF16)
+        rel_cat[:rel_count, layer * breadth : (layer + 1) * breadth] = rel_ref[:, layer, :]
         w_cat[layer, :breadth, :] = wm_ref[layer]
         w_cat[layer, breadth:, :] = ws_ref[layer]
     down = jnp.concatenate(
@@ -308,11 +304,10 @@
         return dot_nt(rounded, w_cat[layer])
 
     def edge_products(kept, cols, layer):
-        @pl.loop(0, chunks)
-        def _(r):
-            grad = dagg[pl.ds(pl.multiple_of(r * STEP, STEP), STEP), :]
+        def piece(r, first):
+            grad = dagg[pl.ds(first(r * STEP), STEP), :]
             for k in range(degree):
-                span = pl.ds(pl.multiple_of(r * group + k * STEP, STEP), STEP)
+                span = pl.ds(first(r * group + k * STEP), STEP)
                 product = kept[span, cols].astype(F32) * grad
                 total = product[:, :breadth]
                 for part in range(1, WIDE // breadth):
@@ -323,6 +318,15 @@
                     contrib[span, :] = (
                         grad * jnp.concatenate([factor] * (WIDE // breadth), axis=1)
                     ).astype(BF16)
+
+        if layer == 1:
+            for r in range(chunks):
+                piece(r, lambda row: row)
+        else:
+
+            @pl.loop(0, chunks)
+            def _(r):
+                piece(r, lambda row: pl.multiple_of(row, STEP))
 
     for half in range(2):
         arrive(0, half)
@@ -513,10 +517,10 @@
     whole = pltpu.make_async_copy(final_in, final_out, copy_sem)
     whole.start()
     breadth = gm_ref.shape[1]
-    rel_count = gr_ref.shape[0] // 2
+    rel_count = gr_ref.shape[0]
     rel_rows = -(-rel_count // 128) * 128
     for layer in range(2):
-        gr_ref[pl.ds(layer, rel_count, stride=2), :] = grads_in[layer, :rel_count, :].astype(F32)
+        gr_ref[:, layer, :] = grads_in[layer, :rel_count, :].astype(F32)
         gm_ref[layer] = grads_in[layer, rel_rows : rel_rows + breadth, :].astype(F32)
         gs_ref[layer] = grads_in[layer, rel_rows + breadth : rel_rows + 2 * breadth, :].astype(F32)
         first = rel_rows + 2 * breadth
@@ -559,7 +563,7 @@
         jax.ShapeDtypeStruct((layers, breadth, breadth), F32),
         jax.ShapeDtypeStruct((layers, breadth), F32),
         jax.ShapeDtypeStruct((layers, breadth), F32),
-        jax.ShapeDtypeStruct((layers * rel_count, breadth), F32),
+        jax.ShapeDtypeStruct((rel_count, layers, breadth), F32),
     ]
     scratch = [
         pltpu.VMEM((layers, 2, rows + slots, half_cols), BF16),
@@ -568,7 +572,6 @@
         pltpu.VMEM((rel_rows, edges), BF16),
         pltpu.VMEM((edges, layers * breadth), BF16),
         pltpu.VMEM((rel_rows, layers * breadth), BF16),
-        pltpu.VMEM((layers * rel_count, breadth), F32),
         pltpu.VMEM((layers, 2 * breadth, breadth), BF16),
         pltpu.VMEM((slots, rows), BF16),
         pltpu.VMEM((rows, slots), BF16),
@@ -619,7 +622,7 @@
         self_weight,
         pre_bias,
         norm_gain,
-        jnp.transpose(rel_embed, (1, 0, 2)).reshape(layers * rel_count, breadth),
+        jnp.transpose(rel_embed, (1, 0, 2)),
         rel_ids.T,
         neighbours.T,
         border,
@@ -631,10 +634,10 @@
         in_specs=[vmem] * 2,
         out_specs=[anywhere] + [vmem] * 5,
         scratch_shapes=[pltpu.SemaphoreType.DMA],
-        compiler_params=pltpu.CompilerParams(vmem_limit_bytes=16 * 1024 * 1024),
+        compiler_params=pltpu.CompilerParams(vmem_limit_bytes=67043328),
         name="unpack",
     )(final, grads)
-    return final, gm, gs, gb, gg, jnp.transpose(gr.reshape(rel_count, layers, breadth), (1, 0, 2))
+    return final, gm, gs, gb, gg, jnp.transpose(gr, (1, 0, 2))
 
 
 def solution(mesh):

time: 94.8 us -> 89.4 us (0.943)
  local copies, waits for them, and re-layouts: 6.08 us -> 0 us
    reshape x2 -> x0, local copies, waits for them, and re-layouts: 3.77 us -> none  [the longest x1 2.38 us: local(): jnp.transpose(rel_embed, (1, 0, 2)).reshape(layers * rel_count, breadth)]
    unnamed x4 -> x0, local copies, waits for them, and re-layouts: 2.3 us -> none
    pallas_call x1, Pallas kernels: 1.68 us -> 3.37 us  [local(): pl.pallas_call(unpack, out_shape=out_shape, in_specs=[vmem] * 2, out_spec...]
    pallas_call x1, Pallas kernels: 86.1 us -> 85 us  [local(): pl.pallas_call(functools.partial(kernel, parts, groups, chunk), out_shape...]
where the time goes in v3:
time: 89.4 us; the launch traced here: 89.2 us
  Pallas kernels  88.4 us (99%)
    pallas_call x1, Pallas kernels, local(): pl.pallas_call(functools.partial(kernel, parts, groups, chunk), out_shape...  85 us
    pallas_call x1, Pallas kernels, local(): pl.pallas_call(unpack, out_shape=out_shape, in_specs=[vmem] * 2, out_spec...  3.37 us

profile of v3, /device:TPU:1, one launch (start us, length us, event | category | flops | bytes accessed | tf_op | source)
XLA Modules:
  0.0 89.2 jit_solution(3846771455009639848)
XLA Ops:
  0.6 85.0 %bellman_ford.1 = (bf16[256,2048]{1,0:T(8,128)(2,1)}, bf16[2,1280,128]{2,1,0:T(8,128)(2,1)}) custom-call(bf16[256,2048]{1,0:T(8,128)(2,1)} %h_ref.1, bf16[256,2048]{1,0:T(8,128)(2,1)} %cot_ref.1, bf16[2,128,128]{2,1,0:T(8,128)(2,1)} %wm_ref.1, bf16[2,128,128]{2,1,0:T(8,128)(2,1)} %ws_ref.1, f32[2,128]{1,0:T(2,128)} %bias_ref.1, f32[2,128]{1,0:T(2,128)} %gain_ref.1, ...), custom_call_target="tpu_custom_call" | custom-call | tf_op jit(solution)/shard_map/bellman_ford/pallas_call | solution.py:608
  85.7 3.4 %unpack.1 = (bf16[256,2048]{1,0:T(8,128)(2,1)}, f32[2,128,128]{2,1,0:T(8,128)}, f32[2,128,128]{2,1,0:T(8,128)}, f32[2,128]{1,0:T(2,128)}, f32[2,128]{1,0:T(2,128)}, /*index=5*/f32[822,2,128]{2,1,0:T(2,128)}) custom-call(bf16[256,2048]{1,0:T(8,128)(2,1)} %get-tuple-element.14.final_in, bf16[2,1280,128]{2,1,0:T(8,128)(2,1)} %get-tuple-element.15.grads_in), custom_call_target="tpu_custom_call" | custom-call | tf_op jit(solution)/shard_map/unpack/pallas_call | solution.py:631
